TPU v7x, 512 devices: a whole 4x8x8 slice. The times are simulated.
512 devices in a mesh: star: 16 (over y, core), cad: 32 (over z, x).
Axes of the slice: x: 4, y: 8, z: 8, core: 2. Of those that a mesh axis runs over, the one named last changes fastest.
Arguments:
- light: float32 [65536, 8192], P('star', 'cad'), may hold values from -2000 to 2000
- quality: int32 [8192], P('cad'), may hold values 0 or 1
- star_factors: float32 [65536, 128], P('star', 'cad'), may hold values from -6 to 6
- cadence_factors: float32 [8192, 128], P('cad', 'star'), may hold values from -6 to 6
Outputs:
- star_gradient: float32 [65536, 128], P('star', 'cad')
- cadence_gradient: float32 [8192, 128], P('cad', 'star')
- loss: float32 [], replicated
All inputs are finite; a program needn't handle non-finite values. No bound on the sum of `quality` on one device may be relied on, other than what follows from the above.
Results may differ from a plain program's by a relative error of at most 0.0003.
Values sent between devices are 32-bit elements; how exact they have to be, the bound alone decides.
A program may use at most 64 MiB of HBM per device.

v0:
```python
import jax
import jax.numpy as jnp
from jax import lax
from jax.sharding import PartitionSpec as P


def on_device(light, quality, star_factors, cadence_factors):
    star_count = light.shape[0] * lax.axis_size("star")
    cad_count = light.shape[1] * lax.axis_size("cad")
    star_loads = lax.all_gather(star_factors, "cad", axis=1, tiled=True)
    cad_loads = lax.all_gather(cadence_factors, "star", axis=1, tiled=True)
    predicted = jnp.dot(
        star_loads, cad_loads.T, precision=lax.Precision.HIGHEST, preferred_element_type=jnp.float32
    )
    residual = light - predicted
    ratio = 1.0 + (residual * 0.5) ** 2
    good = quality.astype(jnp.float32)[None, :]
    weighted = good * residual / ratio
    loss_part = jnp.sum(good * 2.0 * jnp.log(ratio))
    star_term = jnp.dot(
        weighted, cad_loads, precision=lax.Precision.HIGHEST, preferred_element_type=jnp.float32
    )
    cad_term = jnp.dot(
        weighted.T, star_loads, precision=lax.Precision.HIGHEST, preferred_element_type=jnp.float32
    )
    star_width = star_factors.shape[1]
    cad_width = cadence_factors.shape[1]
    star_full, loss_cad = lax.psum((star_term, loss_part), "cad")
    cad_full, loss_all = lax.psum((cad_term, loss_cad), "star")
    star_sum = lax.dynamic_slice_in_dim(
        star_full, lax.axis_index("cad") * star_width, star_width, 1
    )
    cad_sum = lax.dynamic_slice_in_dim(cad_full, lax.axis_index("star") * cad_width, cad_width, 1)
    star_gradient = -star_sum / jnp.sqrt(jnp.float32(cad_count))
    cadence_gradient = -cad_sum / jnp.sqrt(jnp.float32(star_count))
    loss = loss_all / (jnp.float32(star_count) * jnp.float32(cad_count))
    return (star_gradient, cadence_gradient, loss)


def solution(mesh):
    in_specs = (P("star", "cad"), P("cad"), P("star", "cad"), P("cad", "star"))
    out_specs = (P("star", "cad"), P("cad", "star"), P())
    return jax.shard_map(
        on_device, mesh=mesh, in_specs=in_specs, out_specs=out_specs, check_vma=False
    )
```

profile of v0, /device:TPU:8, one launch (start us, length us, event | category | flops | bytes accessed | tf_op | source)
XLA Modules:
  0.0 403.6 jit_solution(11377045682946022342)
XLA Ops:
  7.2 0.0 all-gather.3.cloned.1.call-start
  7.2 0.7 all-gather.3.cloned.1.call-update
  7.9 0.0 all-reduce.5.cloned.1.call-start
  7.9 0.7 convert_element_type.3
  8.6 20.5 %all_gather.7 = f32[256,128]{0,1:T(8,128)S(1)} all-gather(f32[256,8]{0,1:T(8,128)} %param.7), channel_id=1, replica_groups=mesh['star'=16,'cad'=32] {'star'}, dimensions={1}, use_global_device_ids=true | all-gather | bytes 139264 | tf_op jit(solution)/shard_map/all_gather | solution.py:11
  29.1 0.7 broadcast_multiply_fusion
  29.8 70.0 %all-gather.3.cloned.1.call-done = f32[32,4,4096]{2,1,0:T(4,128)} async-done(((f32[1,4,4096]{2,1,0:T(4,128)}), f32[32,4,4096]{2,1,0:T(4,128)}) %all-gather.3.cloned.1.call-update) | async-done | bytes 2097168 | tf_op jit(solution)/shard_map/all_gather | solution.py:10
  99.8 2.0 reshape.10
  101.7 6.7 %multiply_reduce_fusion = (f32[]{:T(128)}, f32[4096,256]{1,0:T(8,128)S(1)}) fusion(f32[256]{0:T(256)S(1)} %broadcast_multiply_fusion, f32[4096,256]{1,0:T(8,128)} %param.4, f32[128,4096]{1,0:T(8,128)S(1)} %reshape.10, f32[256,128]{0,1:T(8,128)S(1)} %all_gather.7), kind=kOutput, calls=%fused_computation.1 | convolution fusion | flops 1616904192 | bytes 10617860 | tf_op jit(solution)/shard_map/dot_general | solution.py:12
  108.5 0.0 copy-start
  108.5 1.9 copy-done
  110.4 4.0 fusion
  114.4 0.0 all-reduce.5.cloned.1.call-update
  114.5 0.0 all-reduce.3.cloned.1.call-start
  114.5 8.8 %fusion.1 = f32[4096,128]{0,1:T(8,128)} fusion(f32[256,128]{0,1:T(8,128)S(1)} %all_gather.7, f32[4096,256]{1,0:T(8,128)} %copy-done, f32[256]{0:T(256)S(1)} %convert_element_type.3), kind=kOutput, calls=%fused_computation.5 | convolution fusion | flops 1615855616 | bytes 6423552 | tf_op jit(solution)/shard_map/dot_general | solution.py:20
  123.3 0.0 all-reduce.3.cloned.1.call-update
  123.3 72.8 %psum.30 = f32[]{:T(128)} all-reduce(f32[]{:T(128)} %get-tuple-element.3), channel_id=1, replica_groups=mesh['star'=16,'cad'=32] {'cad'}, use_global_device_ids=true, to_apply=%region_3.0 | all-reduce | flops 1 | bytes 8 | tf_op jit(solution)/shard_map/psum | solution.py:28
  196.1 21.2 %psum.31 = f32[]{:T(128)} all-reduce(f32[]{:T(128)} %psum.30), channel_id=1, replica_groups=mesh['star'=16,'cad'=32] {'star'}, use_global_device_ids=true, to_apply=%region_4.0 | all-reduce | flops 1 | bytes 8 | tf_op jit(solution)/shard_map/psum | solution.py:29
  217.9 4.7 %all-reduce.5.cloned.1.call-done = f32[256,128]{0,1:T(8,128)} async-done(((f32[256,128]{0,1:T(8,128)}), f32[256,128]{0,1:T(8,128)}) %all-reduce.5.cloned.1.call-update) | async-done | bytes 131088 | tf_op jit(solution)/shard_map/psum | solution.py:29
  222.6 1.3 negate_multiply_fusion.1
  223.9 170.5 %all-reduce.3.cloned.1.call-done = f32[4096,128]{0,1:T(8,128)} async-done(((f32[4096,128]{0,1:T(8,128)}), f32[4096,128]{0,1:T(8,128)}) %all-reduce.3.cloned.1.call-update) | async-done | bytes 2097168 | tf_op jit(solution)/shard_map/psum | solution.py:28
  394.4 1.6 negate_multiply_fusion
Async XLA Ops:
  7.2 92.6 %all-gather.3.cloned.1.call-start = ((), (), s32[]{:S(2)}) async-start(), calls=%async_computation.2 | async-start | bytes 2162688 | tf_op jit(solution)/shard_map/all_gather | solution.py:10
  7.9 214.7 %all-reduce.5.cloned.1.call-start = ((), (), s32[]{:S(2)}) async-start(), calls=%async_computation.1 | async-start | bytes 262144 | tf_op jit(solution)/shard_map/psum | solution.py:29
  108.5 1.9 copy-start
  114.5 279.9 %all-reduce.3.cloned.1.call-start = ((), (), s32[]{:S(2)}) async-start(), calls=%async_computation | async-start | bytes 4194304 | tf_op jit(solution)/shard_map/psum | solution.py:28
Sparse Core Ops, SparseCore 0:
  11.2 88.5 all-gather.2
  114.6 107.9 all-reduce.4
  226.5 167.8 all-reduce.2
where the time goes:
time: 404 us
  waiting for transfers between devices  246 us (61%)
  blocking collectives  114 us (28%)
  matrix products  19.5 us (5%)
  between operations  15.5 us (4%)
  other arithmetic  4.21 us (1%)
    psum x1, waiting for transfers between devices, on_device(): star_full, loss_cad = lax.psum((star_term, loss_part), 'cad')  170 us
    psum x1, blocking collectives, on_device(): star_full, loss_cad = lax.psum((star_term, loss_part), 'cad')  72.8 us
    all_gather x1, waiting for transfers between devices, on_device(): star_loads = lax.all_gather(star_factors, 'cad', axis=1, tiled=True)  70 us
    psum x1, blocking collectives, on_device(): cad_full, loss_all = lax.psum((cad_term, loss_cad), 'star')  21.2 us
    all_gather x1, blocking collectives, on_device(): cad_loads = lax.all_gather(cadence_factors, 'star', axis=1, tiled=True)  20.5 us
    dot_general x1, matrix products, on_device(): jnp.dot(weighted, cad_loads, precision=lax.Precision.HIGHEST, preferred_e...  8.77 us
  transfers between devices with their start and end apart: 3, of which 3 were waited for; matrix products, arithmetic and copies ran while one was open for 3% of the time, Pallas kernels for 0%

commit v1 on v0

--- a/solution.py
+++ b/solution.py
@@ -4,11 +4,29 @@
 from jax.sharding import PartitionSpec as P
 
 
+def in_order(blocks, dim):
+    dims = list(blocks.shape[1:])
+    dims[dim] *= blocks.shape[0]
+    return jnp.moveaxis(blocks, 0, dim).reshape(dims)
+
+
 def on_device(light, quality, star_factors, cadence_factors):
     star_count = light.shape[0] * lax.axis_size("star")
     cad_count = light.shape[1] * lax.axis_size("cad")
     star_loads = lax.all_gather(star_factors, "cad", axis=1, tiled=True)
-    cad_loads = lax.all_gather(cadence_factors, "star", axis=1, tiled=True)
+    size = lax.axis_size("star")
+    pairs = [(i, (i + 1) % size) for i in range(size)]
+    back = [(b, a) for a, b in pairs]
+    lower, upper = ([], [])
+    for step in range(size - 1):
+        if step % 2 == 0:
+            lower.append(lax.ppermute(lower[-1] if lower else cadence_factors, "star", pairs))
+        else:
+            upper.append(lax.ppermute(upper[-1] if upper else cadence_factors, "star", back))
+    blocks = jnp.stack([*lower[::-1], cadence_factors, *upper])
+    shift = lax.axis_index("star") - len(lower)
+    blocks = blocks[(jnp.arange(size) - shift) % size]
+    cad_loads = in_order(blocks, 1)
     predicted = jnp.dot(
         star_loads, cad_loads.T, precision=lax.Precision.HIGHEST, preferred_element_type=jnp.float32
     )

time: 404 us -> 411 us (1.017)
  starting transfers between devices: 0.12 us -> 21.7 us
  blocking collectives: 114 us -> 94 us
  local copies, waits for them, and re-layouts: 3.9 us -> 10.2 us
    ppermute x0 -> x15, starting transfers between devices: none -> 21.5 us  [the longest x7 21.5 us: on_device(): lax.ppermute(upper[-1] if upper else cadence_factors, 'star', back)]
    all_gather x1 -> x0, blocking collectives: 20.5 us -> none  [on_device(): cad_loads = lax.all_gather(cadence_factors, 'star', axis=1, tiled=True)]
    all_gather x1, waiting for transfers between devices: 70 us -> 57 us  [on_device(): star_loads = lax.all_gather(star_factors, 'cad', axis=1, tiled=True)]
    ppermute x0 -> x15, waiting for transfers between devices: none -> 11.5 us  [the longest x8 8.55 us: on_device(): lax.ppermute(lower[-1] if lower else cadence_factors, 'star', pairs)]
    unnamed x3 -> x21, local copies, waits for them, and re-layouts: 3.9 us -> 9.6 us
  transfers between devices with their start and end apart: 3 -> 18, of which waited for: 3 -> 15; matrix products, arithmetic and copies ran while one was open for 3% -> 4% of each run, Pallas kernels for 0% -> 0%
where the time goes in v1:
time: 411 us
  waiting for transfers between devices  246 us (60%)
  blocking collectives  94 us (23%)
  starting transfers between devices  21.7 us (5%)
  matrix products  19.2 us (5%)
  between operations  15.7 us (4%)
  local copies, waits for them, and re-layouts  10.2 us (2%)
  other arithmetic  4.23 us (1%)
    psum x1, waiting for transfers between devices, on_device(): star_full, loss_cad = lax.psum((star_term, loss_part), 'cad')  171 us
    psum x1, blocking collectives, on_device(): star_full, loss_cad = lax.psum((star_term, loss_part), 'cad')  72.8 us
    all_gather x1, waiting for transfers between devices, on_device(): star_loads = lax.all_gather(star_factors, 'cad', axis=1, tiled=True)  57 us
    ppermute x7, starting transfers between devices, on_device(): lax.ppermute(upper[-1] if upper else cadence_factors, 'star', back)  21.5 us
    psum x1, blocking collectives, on_device(): cad_full, loss_all = lax.psum((cad_term, loss_cad), 'star')  21.2 us
    unnamed x21, local copies, waits for them, and re-layouts  9.6 us
    ppermute x8, waiting for transfers between devices, on_device(): lax.ppermute(lower[-1] if lower else cadence_factors, 'star', pairs)  8.55 us
  transfers between devices with their start and end apart: 18, of which 15 were waited for; matrix products, arithmetic and copies ran while one was open for 4% of the time, Pallas kernels for 0%

profile of v1, /device:TPU:8, one launch (start us, length us, event | category | flops | bytes accessed | tf_op | source)
XLA Modules:
  0.0 410.7 jit_solution(4596496890032062473)
XLA Ops:
  7.2 0.0 all-gather.3.cloned.1.call-start
  7.2 0.0 collective-permute-start
  7.2 3.3 collective-permute-done
  10.5 0.0 collective-permute-start.1
  10.5 3.5 collective-permute-start.8
  14.0 1.3 collective-permute-done.1
  15.4 0.0 collective-permute-start.2
  15.4 0.0 all-gather.3.cloned.1.call-update
  15.4 0.0 all-reduce.5.cloned.1.call-start
  15.4 0.2 collective-permute-done.8
  15.6 3.1 collective-permute-start.9
  18.7 1.0 collective-permute-done.2
  19.7 0.0 collective-permute-start.3
  19.7 0.4 collective-permute-done.9
  20.1 3.0 collective-permute-start.10
  23.0 0.9 collective-permute-done.3
  23.9 0.0 collective-permute-start.4
  23.9 0.4 collective-permute-done.10
  24.4 2.9 collective-permute-start.11
  27.3 0.9 collective-permute-done.4
  28.2 0.7 broadcast_multiply_fusion
  28.9 0.0 collective-permute-done.11
  28.9 3.0 collective-permute-start.12
  31.9 0.6 collective-permute-done.5
  32.5 0.0 collective-permute-start.6
  32.5 0.7 collective-permute-done.12
  33.2 3.1 collective-permute-start.13
  36.3 0.5 collective-permute-done.6
  36.8 0.7 convert_element_type.3
  37.5 5.6 %copy.8 = f32[4096,256]{0,1:T(8,128)} copy(f32[4096,256]{1,0:T(8,128)} %param.4) | data formatting | bytes 8388608 | tf_op args[0]
  43.2 3.0 collective-permute-start.14
  46.3 1.2 collective-permute-done.14
  47.5 0.6 gather_fusion
  48.1 57.0 %all-gather.3.cloned.1.call-done = f32[32,4,4096]{2,1,0:T(4,128)} async-done(((f32[1,4,4096]{2,1,0:T(4,128)}), f32[32,4,4096]{2,1,0:T(4,128)}) %all-gather.3.cloned.1.call-update) | async-done | bytes 2097168 | tf_op jit(solution)/shard_map/all_gather | solution.py:16
  105.1 2.0 reshape.71
  107.1 7.0 %multiply_reduce_fusion = (f32[]{:T(128)}, f32[4096,256]{0,1:T(8,128)S(1)}) fusion(f32[256]{0:T(256)S(1)} %broadcast_multiply_fusion, f32[4096,256]{0,1:T(8,128)} %copy.8, f32[128,4096]{1,0:T(8,128)S(1)} %reshape.71, f32[16,256,8]{1,2,0:T(8,128)S(1)} %gather_fusion), kind=kOutput, calls=%fused_computation.3 | convolution fusion | flops 1616904192 | bytes 10617860 | tf_op jit(solution)/shard_map/dot_general | solution.py:30
  114.0 1.9 copy-done
  116.0 5.4 %fusion.6 = f32[256,128]{0,1:T(8,128)} fusion(f32[128,4096]{1,0:T(8,128)S(1)} %reshape.71, f32[4096,256]{0,1:T(8,128)S(1)} %get-tuple-element.4, f32[256]{0:T(256)S(1)} %convert_element_type.3), kind=kOutput, calls=%fused_computation.35 | convolution fusion | flops 1615855616 | bytes 6423552 | tf_op jit(solution)/shard_map/dot_general | solution.py:41
  121.4 0.0 all-reduce.5.cloned.1.call-update
  121.4 0.0 all-reduce.3.cloned.1.call-start
  121.5 6.8 %fusion.1 = f32[4096,128]{0,1:T(8,128)} fusion(f32[16,256,8]{1,2,0:T(8,128)S(1)} %gather_fusion, f32[4096,256]{0,1:T(8,128)} %copy-done, f32[256]{0:T(256)S(1)} %convert_element_type.3), kind=kOutput, calls=%fused_computation.6 | convolution fusion | flops 1615855616 | bytes 6423552 | tf_op jit(solution)/shard_map/dot_general | solution.py:38
  128.3 0.0 all-reduce.3.cloned.1.call-update
  128.3 72.8 %psum.30 = f32[]{:T(128)} all-reduce(f32[]{:T(128)} %get-tuple-element.3), channel_id=1, replica_groups=mesh['star'=16,'cad'=32] {'cad'}, use_global_device_ids=true, to_apply=%region_3.4 | all-reduce | flops 1 | bytes 8 | tf_op jit(solution)/shard_map/psum | solution.py:46
  201.1 21.2 %psum.31 = f32[]{:T(128)} all-reduce(f32[]{:T(128)} %psum.30), channel_id=1, replica_groups=mesh['star'=16,'cad'=32] {'star'}, use_global_device_ids=true, to_apply=%region_4.5 | all-reduce | flops 1 | bytes 8 | tf_op jit(solution)/shard_map/psum | solution.py:47
  223.0 6.6 %all-reduce.5.cloned.1.call-done = f32[256,128]{0,1:T(8,128)} async-done(((f32[256,128]{0,1:T(8,128)}), f32[256,128]{0,1:T(8,128)}) %all-reduce.5.cloned.1.call-update) | async-done | bytes 131088 | tf_op jit(solution)/shard_map/psum | solution.py:47
  229.6 1.3 negate_multiply_fusion.1
  230.9 170.6 %all-reduce.3.cloned.1.call-done = f32[4096,128]{0,1:T(8,128)} async-done(((f32[4096,128]{0,1:T(8,128)}), f32[4096,128]{0,1:T(8,128)}) %all-reduce.3.cloned.1.call-update) | async-done | bytes 2097168 | tf_op jit(solution)/shard_map/psum | solution.py:46
  401.5 1.6 negate_multiply_fusion
  (25 shorter events, 0.1 us)
Async XLA Ops:
  7.2 97.9 %all-gather.3.cloned.1.call-start = ((), (), s32[]{:S(2)}) async-start(), calls=%async_computation.2 | async-start | bytes 2162688 | tf_op jit(solution)/shard_map/all_gather | solution.py:16
  7.2 3.3 collective-permute-start
  10.5 4.9 %collective-permute-start.1 = (f32[256,8]{0,1:T(8,128)S(1)}, f32[256,8]{0,1:T(8,128)S(1)}, u32[]{:S(2)}, u32[]{:S(2)}) collective-permute-start(f32[256,8]{0,1:T(8,128)S(1)} %collective-permute-done), channel_id=1, source_target_pairs={{0,32},{32,64},{64,96},{96,128},{128,160},{160,192},{192,224},{224... | collective-permute-start | bytes 24584 | tf_op jit(solution)/shard_map/ppermute | solution.py:23
  10.5 5.1 %collective-permute-start.8 = (f32[256,8]{0,1:T(8,128)}, f32[256,8]{0,1:T(8,128)S(1)}, u32[]{:S(2)}, u32[]{:S(2)}) collective-permute-start(f32[256,8]{0,1:T(8,128)} %param.7), channel_id=1, source_target_pairs={{32,0},{64,32},{96,64},{128,96},{160,128},{192,160},{224,192},{256... | collective-permute-start | bytes 24584 | tf_op jit(solution)/shard_map/ppermute | solution.py:25
  15.4 4.3 %collective-permute-start.2 = (f32[256,8]{0,1:T(8,128)S(1)}, f32[256,8]{0,1:T(8,128)S(1)}, u32[]{:S(2)}, u32[]{:S(2)}) collective-permute-start(f32[256,8]{0,1:T(8,128)S(1)} %collective-permute-done.1), channel_id=1, source_target_pairs={{0,32},{32,64},{64,96},{96,128},{128,160},{160,192},{192,224},{224... | collective-permute-start | bytes 24584 | tf_op jit(solution)/shard_map/ppermute | solution.py:23
  15.4 214.2 %all-reduce.5.cloned.1.call-start = ((), (), s32[]{:S(2)}) async-start(), calls=%async_computation.1 | async-start | bytes 262144 | tf_op jit(solution)/shard_map/psum | solution.py:47
  15.6 4.4 %collective-permute-start.9 = (f32[256,8]{0,1:T(8,128)S(1)}, f32[256,8]{0,1:T(8,128)S(1)}, u32[]{:S(2)}, u32[]{:S(2)}) collective-permute-start(f32[256,8]{0,1:T(8,128)S(1)} %collective-permute-done.8), channel_id=1, source_target_pairs={{32,0},{64,32},{96,64},{128,96},{160,128},{192,160},{224,192},{256... | collective-permute-start | bytes 24584 | tf_op jit(solution)/shard_map/ppermute | solution.py:25
  19.7 4.3 %collective-permute-start.3 = (f32[256,8]{0,1:T(8,128)S(1)}, f32[256,8]{0,1:T(8,128)S(1)}, u32[]{:S(2)}, u32[]{:S(2)}) collective-permute-start(f32[256,8]{0,1:T(8,128)S(1)} %collective-permute-done.2), channel_id=1, source_target_pairs={{0,32},{32,64},{64,96},{96,128},{128,160},{160,192},{192,224},{224... | collective-permute-start | bytes 24584 | tf_op jit(solution)/shard_map/ppermute | solution.py:23
  20.1 4.3 %collective-permute-start.10 = (f32[256,8]{0,1:T(8,128)S(1)}, f32[256,8]{0,1:T(8,128)S(1)}, u32[]{:S(2)}, u32[]{:S(2)}) collective-permute-start(f32[256,8]{0,1:T(8,128)S(1)} %collective-permute-done.9), channel_id=1, source_target_pairs={{32,0},{64,32},{96,64},{128,96},{160,128},{192,160},{224,192},{256... | collective-permute-start | bytes 24584 | tf_op jit(solution)/shard_map/ppermute | solution.py:25
  23.9 4.3 %collective-permute-start.4 = (f32[256,8]{0,1:T(8,128)S(1)}, f32[256,8]{0,1:T(8,128)S(1)}, u32[]{:S(2)}, u32[]{:S(2)}) collective-permute-start(f32[256,8]{0,1:T(8,128)S(1)} %collective-permute-done.3), channel_id=1, source_target_pairs={{0,32},{32,64},{64,96},{96,128},{128,160},{160,192},{192,224},{224... | collective-permute-start | bytes 24584 | tf_op jit(solution)/shard_map/ppermute | solution.py:23
  24.4 4.5 %collective-permute-start.11 = (f32[256,8]{0,1:T(8,128)S(1)}, f32[256,8]{0,1:T(8,128)S(1)}, u32[]{:S(2)}, u32[]{:S(2)}) collective-permute-start(f32[256,8]{0,1:T(8,128)S(1)} %collective-permute-done.10), channel_id=1, source_target_pairs={{32,0},{64,32},{96,64},{128,96},{160,128},{192,160},{224,192},{256... | collective-permute-start | bytes 24584 | tf_op jit(solution)/shard_map/ppermute | solution.py:25
  28.2 4.3 %collective-permute-start.5 = (f32[256,8]{0,1:T(8,128)S(1)}, f32[256,8]{0,1:T(8,128)S(1)}, u32[]{:S(2)}, u32[]{:S(2)}) collective-permute-start(f32[256,8]{0,1:T(8,128)S(1)} %collective-permute-done.4), channel_id=1, source_target_pairs={{0,32},{32,64},{64,96},{96,128},{128,160},{160,192},{192,224},{224... | collective-permute-start | bytes 24584 | tf_op jit(solution)/shard_map/ppermute | solution.py:23
  28.9 4.3 %collective-permute-start.12 = (f32[256,8]{0,1:T(8,128)S(1)}, f32[256,8]{0,1:T(8,128)S(1)}, u32[]{:S(2)}, u32[]{:S(2)}) collective-permute-start(f32[256,8]{0,1:T(8,128)S(1)} %collective-permute-done.11), channel_id=1, source_target_pairs={{32,0},{64,32},{96,64},{128,96},{160,128},{192,160},{224,192},{256... | collective-permute-start | bytes 24584 | tf_op jit(solution)/shard_map/ppermute | solution.py:25
  32.5 4.3 %collective-permute-start.6 = (f32[256,8]{0,1:T(8,128)S(1)}, f32[256,8]{0,1:T(8,128)S(1)}, u32[]{:S(2)}, u32[]{:S(2)}) collective-permute-start(f32[256,8]{0,1:T(8,128)S(1)} %collective-permute-done.5), channel_id=1, source_target_pairs={{0,32},{32,64},{64,96},{96,128},{128,160},{160,192},{192,224},{224... | collective-permute-start | bytes 24584 | tf_op jit(solution)/shard_map/ppermute | solution.py:23
  33.2 9.9 %collective-permute-start.13 = (f32[256,8]{0,1:T(8,128)S(1)}, f32[256,8]{0,1:T(8,128)S(1)}, u32[]{:S(2)}, u32[]{:S(2)}) collective-permute-start(f32[256,8]{0,1:T(8,128)S(1)} %collective-permute-done.12), channel_id=1, source_target_pairs={{32,0},{64,32},{96,64},{128,96},{160,128},{192,160},{224,192},{256... | collective-permute-start | bytes 24584 | tf_op jit(solution)/shard_map/ppermute | solution.py:25
  36.8 9.3 %collective-permute-start.7 = (f32[256,8]{0,1:T(8,128)S(1)}, f32[256,8]{0,1:T(8,128)S(1)}, u32[]{:S(2)}, u32[]{:S(2)}) collective-permute-start(f32[256,8]{0,1:T(8,128)S(1)} %collective-permute-done.6), channel_id=1, source_target_pairs={{0,32},{32,64},{64,96},{96,128},{128,160},{160,192},{192,224},{224... | collective-permute-start | bytes 24584 | tf_op jit(solution)/shard_map/ppermute | solution.py:23
  37.5 8.7 %copy-start.1 = (f32[256,8]{0,1:T(8,128)S(1)}, f32[256,8]{0,1:T(8,128)}, u32[]{:S(2)}) copy-start(f32[256,8]{0,1:T(8,128)} %param.7) | copy-start | bytes 24580
  43.2 4.4 %collective-permute-start.14 = (f32[256,8]{0,1:T(8,128)S(1)}, f32[256,8]{0,1:T(8,128)S(1)}, u32[]{:S(2)}, u32[]{:S(2)}) collective-permute-start(f32[256,8]{0,1:T(8,128)S(1)} %collective-permute-done.13), channel_id=1, source_target_pairs={{32,0},{64,32},{96,64},{128,96},{160,128},{192,160},{224,192},{256... | collective-permute-start | bytes 24584 | tf_op jit(solution)/shard_map/ppermute | solution.py:25
  114.0 2.0 copy-start
  121.4 280.1 %all-reduce.3.cloned.1.call-start = ((), (), s32[]{:S(2)}) async-start(), calls=%async_computation | async-start | bytes 4194304 | tf_op jit(solution)/shard_map/psum | solution.py:46
Sparse Core Ops, SparseCore 0:
  15.5 89.5 all-gather.2
  121.6 108.0 all-reduce.4
  233.6 167.9 all-reduce.2
